TPU v7x, 256 devices: a whole 4x4x8 slice. The times are simulated.
256 devices in a mesh: ctx: 16 (over y, x), head: 4 (over z_hi, core), dp: 4 (over z_lo).
Axes of the slice: x: 4, y: 4, z: 8 (z_hi: 2, z_lo: 4; z = z_hi * 4 + z_lo), core: 2. Of those that a mesh axis runs over, the one named last changes fastest.
Arguments:
- queries: bfloat16 [4096, 8, 8, 128], P('ctx', 'head', 'dp'), may hold values from -2.5 to 2.5
- key_rows: bfloat16 [4096, 8, 128], P(('ctx', 'dp'), 'head'), may hold values from -2.5 to 2.5
- value_rows: bfloat16 [4096, 8, 128], P(('ctx', 'dp'), 'head'), may hold values from -6 to 6
- forward_out: bfloat16 [4096, 8, 8, 128], P('ctx', 'head', 'dp'), may hold values from -0.59765625 to 0.59765625
- grad_out: bfloat16 [4096, 8, 8, 128], P('ctx', 'head', 'dp'), may hold values from -24 to 24
- logsumexp: float32 [8, 8, 4096], P('head', 'dp', 'ctx'), as said below
- selected: int32 [16, 8, 8, 8], P('ctx', 'head', 'dp'), may hold values from -1 to 15, as said below
Outputs:
- query_grad: bfloat16 [4096, 8, 8, 128], P('ctx', 'head', 'dp')
- key_grad: float32 [4096, 8, 128], P(('ctx', 'dp'), 'head')
- value_grad: float32 [4096, 8, 128], P(('ctx', 'dp'), 'head')
Inputs may be any that keep to these rules, and one draw needn't show every extreme that they name: selected[i, a, g, 0] = i. The other entries of a row are distinct blocks below i (some blocks below i may be left out), followed by -1 in the slots that remain. `logsumexp`: each entry lies between log(512) and log(512) + 1.5.
All inputs are finite; a program needn't handle non-finite values.
Results may differ from a plain program's by a relative error of at most 0.0051.
Values may be sent and summed in bfloat16 or wider, within the bound.
No kernel may reach another device: no remote copies, remote signals or barrier semaphores. Data moves between devices by JAX's collectives and lax.ppermute only.
A program may use at most 64 MiB of HBM per device.

v0:
```python
import jax
import jax.numpy as jnp
from jax import lax
from jax.sharding import PartitionSpec as P

BLOCK = 256


def block_terms(
    query_blk,
    grad_blk,
    lse_row,
    delta_part,
    slot_ids,
    key_view,
    value_layout,
    head_local,
    slot_offset,
    softmax_scale,
):
    slot_count = slot_ids.shape[0]
    block_len = query_blk.shape[0]
    safe_ids = jnp.maximum(slot_ids, 0)
    positions = jnp.arange(block_len, dtype=jnp.int32)
    key_sel = key_view[safe_ids[:, None], positions[None, :], head_local].reshape(
        slot_count * block_len, -1
    )
    value_sel = value_layout[safe_ids[:, None], positions[None, :], head_local].reshape(
        slot_count * block_len, -1
    )
    columns = jnp.arange(slot_count * block_len, dtype=jnp.int32)
    slot_of = columns // block_len
    within = columns % block_len
    filled = slot_ids[slot_of] >= 0
    causal = (slot_of + slot_offset != 0)[None, :] | (within[None, :] <= positions[:, None])
    keep = filled[None, :] & causal
    score_rows = (
        lax.dot_general(
            query_blk, key_sel, (((1,), (1,)), ((), ())), preferred_element_type=jnp.float32
        )
        * softmax_scale
    )
    probs = jnp.where(keep, jnp.exp(score_rows - lse_row[:, None]), jnp.float32(0.0))
    probs_low = probs.astype(jnp.bfloat16)
    value_part = lax.dot_general(
        probs_low, grad_blk, (((0,), (0,)), ((), ())), preferred_element_type=jnp.float32
    )
    dprobs = lax.dot_general(
        grad_blk, value_sel, (((1,), (1,)), ((), ())), preferred_element_type=jnp.float32
    )
    dscores = (probs * (dprobs - delta_part[:, None]) * softmax_scale).astype(jnp.bfloat16)
    query_part = jnp.dot(dscores, key_sel, preferred_element_type=jnp.float32)
    key_part = lax.dot_general(
        dscores, query_blk, (((0,), (0,)), ((), ())), preferred_element_type=jnp.float32
    )
    return (
        query_part,
        key_part.reshape(slot_count, block_len, -1),
        value_part.reshape(slot_count, block_len, -1),
    )


def local(queries, key_rows, value_rows, forward_out, grad_out, logsumexp, selected):
    rows_local, kv_local, group_local, head_dim = queries.shape
    blocks_local = selected.shape[0]
    slot_total = selected.shape[3]
    half_slots = slot_total // 2
    softmax_scale = head_dim ** (-0.5)
    keys_all, values_all = (
        lax.all_gather(key_rows, ("ctx", "dp"), axis=0, tiled=True),
        lax.all_gather(value_rows, ("ctx", "dp"), axis=0, tiled=True),
    )
    total_rows = keys_all.shape[0]
    block_total = total_rows // BLOCK
    key_view = keys_all.reshape(block_total, BLOCK, kv_local, head_dim)
    value_layout = values_all.reshape(block_total, BLOCK, kv_local, head_dim)
    positions = jnp.arange(BLOCK, dtype=jnp.int32)
    delta_rows = jnp.sum(grad_out.astype(jnp.float32) * forward_out.astype(jnp.float32), axis=-1)

    def head_step(carried, item_index):
        key_acc, value_acc = carried
        block_index = item_index // (kv_local * group_local)
        head_local = item_index // group_local % kv_local
        group_index = item_index % group_local
        zero_index = jnp.zeros((), jnp.int32)
        row_start = block_index * BLOCK
        query_blk = lax.dynamic_slice(
            queries, (row_start, head_local, group_index, zero_index), (BLOCK, 1, 1, head_dim)
        ).reshape(BLOCK, head_dim)
        grad_blk = lax.dynamic_slice(
            grad_out, (row_start, head_local, group_index, zero_index), (BLOCK, 1, 1, head_dim)
        ).reshape(BLOCK, head_dim)
        lse_row = lax.dynamic_slice(
            logsumexp, (head_local, group_index, row_start), (1, 1, BLOCK)
        ).reshape(BLOCK)
        delta_part = lax.dynamic_slice(
            delta_rows, (row_start, head_local, group_index), (BLOCK, 1, 1)
        ).reshape(BLOCK)
        slot_ids = lax.dynamic_slice(
            selected, (block_index, head_local, group_index, zero_index), (1, 1, 1, slot_total)
        ).reshape(slot_total)
        query_acc = jnp.zeros((BLOCK, head_dim), jnp.float32)
        for half_index in range(2):
            offset = half_index * half_slots
            part_ids = slot_ids[offset : offset + half_slots]
            query_part, key_part, value_part = block_terms(
                query_blk,
                grad_blk,
                lse_row,
                delta_part,
                part_ids,
                key_view,
                value_layout,
                head_local,
                offset,
                softmax_scale,
            )
            target_ids = jnp.where(part_ids >= 0, part_ids, block_total)
            key_acc = key_acc.at[target_ids[:, None], positions[None, :], head_local].add(
                key_part, mode="drop"
            )
            value_acc = value_acc.at[target_ids[:, None], positions[None, :], head_local].add(
                value_part, mode="drop"
            )
            query_acc = query_acc + query_part
        return ((key_acc, value_acc), query_acc.astype(jnp.bfloat16))

    empty = jnp.zeros((block_total, BLOCK, kv_local, head_dim), jnp.float32)
    items = jnp.arange(blocks_local * kv_local * group_local, dtype=jnp.int32)
    (key_acc, value_acc), query_blocks = lax.scan(head_step, (empty, empty), items)
    query_grad = (
        query_blocks.reshape(blocks_local, kv_local, group_local, BLOCK, head_dim)
        .transpose(0, 3, 1, 2, 4)
        .reshape(rows_local, kv_local, group_local, head_dim)
    )
    key_terms = key_acc.reshape(total_rows, kv_local, head_dim)
    value_terms = value_acc.reshape(total_rows, kv_local, head_dim)
    key_grad, value_grad = (
        lax.psum_scatter(key_terms, ("ctx", "dp"), scatter_dimension=0, tiled=True),
        lax.psum_scatter(value_terms, ("ctx", "dp"), scatter_dimension=0, tiled=True),
    )
    return (query_grad, key_grad, value_grad)


def solution(mesh):
    return jax.shard_map(
        local,
        mesh=mesh,
        in_specs=(
            P("ctx", "head", "dp", None),
            P(("ctx", "dp"), "head", None),
            P(("ctx", "dp"), "head", None),
            P("ctx", "head", "dp", None),
            P("ctx", "head", "dp", None),
            P("head", "dp", "ctx"),
            P("ctx", "head", "dp", None),
        ),
        out_specs=(
            P("ctx", "head", "dp", None),
            P(("ctx", "dp"), "head", None),
            P(("ctx", "dp"), "head", None),
        ),
        check_vma=False,
    )
```

profile of v0, /device:TPU:0, one launch (start us, length us, event | category | flops | bytes accessed | tf_op | source)
XLA Modules:
  0.0 1941.0 jit_solution(5706698245401311569)
XLA Ops:
  14.0 347.1 %all-gather.3.cloned.1.call-done = bf16[4096,2,128]{2,1,0:T(2,128)(2,1)} async-done(((bf16[64,2,128]{2,1,0:T(2,128)(2,1)}), bf16[4096,2,128]{2,1,0:T(2,128)(2,1)}) %all-gather.3.cloned.1.call-update) | async-done | bytes 2097168 | tf_op jit(solution)/shard_map/all_gather | solution.py:70
  361.1 349.4 %all-gather.5.cloned.1.call-done = bf16[4096,2,128]{2,1,0:T(2,128)(2,1)} async-done(((bf16[64,2,128]{2,1,0:T(2,128)(2,1)}), bf16[4096,2,128]{2,1,0:T(2,128)(2,1)}) %all-gather.5.cloned.1.call-update) | async-done | bytes 2097168 | tf_op jit(solution)/shard_map/all_gather | solution.py:71
  717.9 441.2 %while.19 = (s32[]{:T(128)}, f32[16,256,2,128]{3,2,1,0:T(2,128)}, f32[16,256,2,128]{3,2,1,0:T(2,128)}, bf16[4,256,128]{2,1,0:T(8,128)(2,1)}, s32[4]{0:T(128)S(1)...) while((s32[]{:T(128)}, f32[16,256,2,128]{3,2,1,0:T(2,128)}, ...), condition=%wide.region_6.7_spmd.clone.clone, body=%wide.region_1.6_spmd.clone.clone.sunk | while | flops 682269824 | bytes 35151920 | solution.py:130
  735.1 12.7 gather_fusion.3
  747.7 6.2 gather_fusion
  753.9 12.7 gather_fusion.2
  789.4 10.0 scatter_fusion.2
  799.4 10.0 scatter_fusion.3
  809.3 9.5 scatter_fusion
  818.8 9.5 scatter_fusion.1
  845.3 12.7 gather_fusion.3
  858.0 6.2 gather_fusion
  864.1 12.7 gather_fusion.2
  899.6 10.0 scatter_fusion.2
  909.6 10.0 scatter_fusion.3
  919.6 9.5 scatter_fusion
  929.1 9.5 scatter_fusion.1
  955.6 12.7 gather_fusion.3
  968.2 6.2 gather_fusion
  974.4 12.7 gather_fusion.2
  1009.9 10.0 scatter_fusion.2
  1019.9 10.0 scatter_fusion.3
  1029.8 9.5 scatter_fusion
  1039.3 9.5 scatter_fusion.1
  1065.8 12.7 gather_fusion.3
  1078.5 6.2 gather_fusion
  1084.6 12.7 gather_fusion.2
  1120.1 10.0 scatter_fusion.2
  1130.1 10.0 scatter_fusion.3
  1140.1 9.5 scatter_fusion
  1149.6 9.5 scatter_fusion.1
  1161.9 771.0 %all-reduce.5.cloned.1.call-done = (f32[4096,2,128]{2,1,0:T(2,128)}, f32[4096,2,128]{2,1,0:T(2,128)}) async-done(((f32[4096,2,128]{2,1,0:T(2,128)}, f32[4096,2,128]{2,1,0:T(2,128)}), (f32[4096,2,128]{2,1,0:T(2,128)}, f32[4096,2,128]{2,1,0:T(2,128)})) %all-reduce.5.cloned.1.call-update) | async-done | bytes 8388624
  (179 shorter events, 166.1 us)
Async XLA Ops:
  7.2 354.0 %all-gather.3.cloned.1.call-start = ((), (), s32[]{:S(2)}) async-start(), calls=%async_computation | async-start | bytes 2129920 | tf_op jit(solution)/shard_map/all_gather | solution.py:70
  7.9 702.6 %all-gather.5.cloned.1.call-start = ((), (), s32[]{:S(2)}) async-start(), calls=%async_computation.1 | async-start | bytes 2129920 | tf_op jit(solution)/shard_map/all_gather | solution.py:71
  8.6 1924.3 %all-reduce.5.cloned.1.call-start = ((), (), s32[]{:S(2)}) async-start(), calls=%async_computation.2 | async-start | bytes 16777216
  710.5 7.4 copy-start
  710.5 7.4 copy-start.3
  710.5 7.4 copy-start.4
  774.2 6.5 copy-start.1
  884.4 6.5 copy-start.1
  994.7 6.5 copy-start.1
  1104.9 6.5 copy-start.1
  1159.1 0.7 copy-start.5
  1159.1 1.9 copy-start.2
Sparse Core Ops, SparseCore 0:
  9.8 351.3 all-gather.2
  362.9 347.5 all-gather.4
  1159.3 773.6 all-reduce.4
where the time goes:
time: 1950 us; the launch traced here: 1940 us
  waiting for transfers between devices  1470 us (75%)
  local copies, waits for them, and re-layouts  205 us (11%)
  other arithmetic  179 us (9%)
  matrix products  62.6 us (3%)
    unnamed x4, waiting for transfers between devices  772 us
    all_gather x1, waiting for transfers between devices, local(): lax.all_gather(value_rows, ('ctx', 'dp'), axis=0, tiled=True)  349 us
    all_gather x1, waiting for transfers between devices, local(): lax.all_gather(key_rows, ('ctx', 'dp'), axis=0, tiled=True)  347 us
    while x32, other arithmetic  157 us
    gather x8, local copies, waits for them, and re-layouts, block_terms(): value_layout[safe_ids[:, None], positions[None, :], head_local]  101 us
    gather x8, local copies, waits for them, and re-layouts, block_terms(): key_view[safe_ids[:, None], positions[None, :], head_local]  49.2 us
  transfers between devices with their start and end apart: 3, of which 3 were waited for; matrix products, arithmetic and copies ran while one was open for 0% of the time, Pallas kernels for 0%

commit v1 on v0

--- a/solution.py
+++ b/solution.py
@@ -67,7 +67,12 @@
     half_slots = slot_total // 2
     softmax_scale = head_dim ** (-0.5)
     keys_all, values_all = (
-        lax.all_gather(key_rows, ("ctx", "dp"), axis=0, tiled=True),
+        jnp.concatenate(
+            lax.all_to_all(
+                jnp.stack([key_rows] * lax.axis_size(("ctx", "dp"))), ("ctx", "dp"), 0, 0
+            ),
+            axis=0,
+        ),
         lax.all_gather(value_rows, ("ctx", "dp"), axis=0, tiled=True),
     )
     total_rows = keys_all.shape[0]

time: 1950 us -> 1600 us (0.82)
  waiting for transfers between devices: 1470 us -> 1110 us
    all_gather x1 -> x0, waiting for transfers between devices: 347 us -> none  [local(): lax.all_gather(key_rows, ('ctx', 'dp'), axis=0, tiled=True)]
    unnamed x4 -> x3, waiting for transfers between devices: 772 us -> 772 us
  transfers between devices with their start and end apart: 3 -> 3, of which waited for: 3 -> 2; matrix products, arithmetic and copies ran while one was open for 0% -> 1% of each run, Pallas kernels for 0% -> 0%
where the time goes in v1:
time: 1600 us; the launch traced here: 1590 us
  waiting for transfers between devices  1110 us (69%)
  local copies, waits for them, and re-layouts  207 us (13%)
  other arithmetic  178 us (11%)
  matrix products  62.4 us (4%)
    unnamed x3, waiting for transfers between devices  772 us
    all_gather x1, waiting for transfers between devices, local(): lax.all_gather(value_rows, ('ctx', 'dp'), axis=0, tiled=True)  338 us
    while x32, other arithmetic  157 us
    gather x8, local copies, waits for them, and re-layouts, block_terms(): value_layout[safe_ids[:, None], positions[None, :], head_local]  101 us
    gather x8, local copies, waits for them, and re-layouts, block_terms(): key_view[safe_ids[:, None], positions[None, :], head_local]  49.2 us
  transfers between devices with their start and end apart: 3, of which 2 were waited for; matrix products, arithmetic and copies ran while one was open for 1% of the time, Pallas kernels for 0%

profile of v1, /device:TPU:0, one launch (start us, length us, event | category | flops | bytes accessed | tf_op | source)
XLA Modules:
  0.0 1593.8 jit_solution(10469738694188776644)
XLA Ops:
  12.0 10.3 all-to-all-start
  24.8 338.1 %all-gather.2.cloned.1.call-done = bf16[4096,2,128]{2,1,0:T(2,128)(2,1)} async-done(((bf16[64,2,128]{2,1,0:T(2,128)(2,1)}), bf16[4096,2,128]{2,1,0:T(2,128)(2,1)}) %all-gather.2.cloned.1.call-update) | async-done | bytes 2097168 | tf_op jit(solution)/shard_map/all_gather | solution.py:76
  370.4 440.5 %while.19 = (s32[]{:T(128)}, f32[16,256,2,128]{3,2,1,0:T(2,128)}, f32[16,256,2,128]{3,2,1,0:T(2,128)}, bf16[4,256,128]{2,1,0:T(8,128)(2,1)}, s32[4]{0:T(128)S(1)...) while((s32[]{:T(128)}, f32[16,256,2,128]{3,2,1,0:T(2,128)}, ...), condition=%wide.region_6.7_spmd.clone.clone, body=%wide.region_1.6_spmd.clone.clone.sunk | while | flops 682269824 | bytes 35151920 | solution.py:135
  387.4 12.6 gather_fusion.3
  400.0 6.2 gather_fusion
  406.1 12.6 gather_fusion.2
  441.5 10.0 scatter_fusion.2
  451.4 10.0 scatter_fusion.3
  461.4 9.6 scatter_fusion
  471.0 9.6 scatter_fusion.1
  497.5 12.6 gather_fusion.3
  510.1 6.2 gather_fusion
  516.2 12.6 gather_fusion.2
  551.6 10.0 scatter_fusion.2
  561.6 10.0 scatter_fusion.3
  571.5 9.6 scatter_fusion
  581.1 9.6 scatter_fusion.1
  607.6 12.6 gather_fusion.3
  620.2 6.2 gather_fusion
  626.4 12.6 gather_fusion.2
  661.7 10.0 scatter_fusion.2
  671.7 10.0 scatter_fusion.3
  681.6 9.6 scatter_fusion
  691.2 9.6 scatter_fusion.1
  717.7 12.6 gather_fusion.3
  730.3 6.2 gather_fusion
  736.5 12.6 gather_fusion.2
  771.8 10.0 scatter_fusion.2
  781.8 10.0 scatter_fusion.3
  791.7 9.6 scatter_fusion
  801.3 9.6 scatter_fusion.1
  813.7 771.7 %all-reduce.5.cloned.1.call-done = (f32[4096,2,128]{2,1,0:T(2,128)}, f32[4096,2,128]{2,1,0:T(2,128)}) async-done(((f32[4096,2,128]{2,1,0:T(2,128)}, f32[4096,2,128]{2,1,0:T(2,128)}), (f32[4096,2,128]{2,1,0:T(2,128)}, f32[4096,2,128]{2,1,0:T(2,128)})) %all-reduce.5.cloned.1.call-update) | async-done | bytes 8388624
  (183 shorter events, 166.4 us)
Async XLA Ops:
  7.2 15.2 copy-start.3
  7.2 15.9 copy-start.1
  7.2 16.7 %copy-start.2 = (bf16[256,2,2,128]{3,2,1,0:T(2,128)(2,1)S(1)}, bf16[256,2,2,128]{3,2,1,0:T(2,128)(2,1)}, u32[]{:S(2)}) copy-start(bf16[256,2,2,128]{3,2,1,0:T(2,128)(2,1)} %param.12) | copy-start | bytes 786436
  7.2 355.8 %all-gather.2.cloned.1.call-start = ((), (), s32[]{:S(2)}) async-start(), calls=%async_computation.1 | async-start | bytes 2129920 | tf_op jit(solution)/shard_map/all_gather | solution.py:76
  12.0 351.0 %all-to-all-start = ((bf16[64,64,2,128]{3,2,1,0:T(2,128)(2,1)}), bf16[64,64,2,128]{3,2,1,0:T(2,128)(2,1)S(1)}, u32[]{:S(2)}, u32[]{:S(2)}) async-start(bf16[64,64,2,128]{3,2,1,0:T(2,128)(2,1)} %stack.2), calls=%async_computation | async-start | bytes 4194304 | tf_op jit(solution)/shard_map/all_to_all | solution.py:71
  22.3 1563.1 %all-reduce.5.cloned.1.call-start = ((), (), s32[]{:S(2)}) async-start(), calls=%async_computation.2 | async-start | bytes 16777216
  363.0 7.4 copy-start.5
  363.0 7.4 copy-start.6
  426.3 6.5 copy-start
  536.4 6.5 copy-start
  646.5 6.5 copy-start
  756.7 6.5 copy-start
  810.9 0.7 copy-start.7
  810.9 1.9 copy-start.4
Sparse Core Ops, SparseCore 0:
  9.8 353.1 all-gather.1
  811.0 774.3 all-reduce.4
